TPU v7x, 32 devices: a whole 2x2x4 slice. The times are simulated.
32 devices in a mesh: dp: 8 (over z, x), seq: 4 (over y, core).
Axes of the slice: x: 2, y: 2, z: 4, core: 2. Of those that a mesh axis runs over, the one named last changes fastest.
Arguments:
- layer_input: bfloat16 [16, 1024, 512], P('dp', 'seq'), may hold values from -6 to 6
- memory: bfloat16 [16, 1024, 512], P('dp', 'seq'), may hold values from -6 to 6
- timesteps: int32 [16], P('dp'), may hold values from 0 to 49
- upstream: bfloat16 [16, 1024, 512], P('dp', 'seq'), may hold values from -6 to 6
- step_table: bfloat16 [50, 512], replicated, may hold values from -3 to 3
- norm_gains: float32 [3, 512], replicated, may hold values from 0.5 to 1.5
- shift_rows: float32 [10, 512], replicated, may hold values from -1.8 to 1.8
- self_entry: bfloat16 [512, 1536], replicated, may hold values from -0.25 to 0.25
- self_exit: bfloat16 [512, 512], replicated, may hold values from -4 to 4
- cross_query: bfloat16 [512, 512], replicated, may hold values from -0.25 to 0.25
- cross_keyval: bfloat16 [512, 1024], replicated, may hold values from -0.25 to 0.25
- cross_exit: bfloat16 [512, 512], replicated, may hold values from -4 to 4
- expand_weight: bfloat16 [512, 2048], replicated, may hold values from -0.25 to 0.25
- expand_bias: float32 [2048], replicated, may hold values from -1.8 to 1.8
- reduce_weight: bfloat16 [2048, 512], replicated, may hold values from -0.125 to 0.125
Outputs:
- result: float32 [16, 1024, 512], P('dp', 'seq')
- input_gradient: float32 [16, 1024, 512], P('dp', 'seq')
- memory_gradient: float32 [16, 1024, 512], P('dp', 'seq')
- table_gradient: float32 [50, 512], replicated
- gains_gradient: float32 [3, 512], replicated
- shifts_gradient: float32 [10, 512], replicated
- entry_gradient: float32 [512, 1536], replicated
- self_exit_gradient: float32 [512, 512], replicated
- cross_query_gradient: float32 [512, 512], replicated
- cross_keyval_gradient: float32 [512, 1024], replicated
- cross_exit_gradient: float32 [512, 512], replicated
- expand_gradient: float32 [512, 2048], replicated
- expand_bias_gradient: float32 [2048], replicated
- reduce_gradient: float32 [2048, 512], replicated
All inputs are finite; a program needn't handle non-finite values.
Results may differ from a plain program's by a relative error of at most 0.017.
Values may be sent and summed in bfloat16 or wider, within the bound.
No kernel may reach another device: no remote copies, remote signals or barrier semaphores. Data moves between devices by JAX's collectives and lax.ppermute only.
A program may use at most 192 MiB of HBM per device.

v0:
```python
import math

import jax
import jax.numpy as jnp
from jax import lax
from jax.sharding import PartitionSpec as P

H = 8
HD = 64


EPSILON = 1e-05


def layer_norm(values, norm_gain, norm_shift):
    centered = values - jnp.mean(values, axis=-1, keepdims=True)
    inverse = lax.rsqrt(jnp.mean(centered * centered, axis=-1, keepdims=True) + EPSILON)
    return centered * inverse * norm_gain + norm_shift


def norm_back(values, norm_gain, norm_shift, incoming):
    _, pullback = jax.vjp(layer_norm, values, norm_gain, norm_shift)
    return pullback(incoming)


def gelu_tanh(values):
    return jax.nn.gelu(values, approximate=True)


def project(row_block, weight):
    return jnp.einsum("sqd,de->sqe", row_block, weight, preferred_element_type=jnp.float32)


def project_back(grad_block, weight):
    return jnp.einsum("sqe,de->sqd", grad_block, weight, preferred_element_type=jnp.float32)


def weight_grad(row_block, grad_block):
    return jnp.einsum("sqd,sqe->de", row_block, grad_block, preferred_element_type=jnp.float32)


def column_sums(grad_block):
    return jnp.sum(grad_block.astype(jnp.float32), axis=(0, 1))


def split_heads(row_block):
    return row_block.reshape(row_block.shape[0], row_block.shape[1], H, HD)


def score_block(queries, keys):
    scaling = 1.0 / math.sqrt(HD)
    return (
        jnp.einsum(
            "sqhd,skhd->shqk",
            split_heads(queries),
            split_heads(keys),
            preferred_element_type=jnp.float32,
        )
        * scaling
    )


def attend(queries, keys, values):
    scores = score_block(queries, keys)
    row_max = jnp.max(scores, axis=-1, keepdims=True)
    exponent = jnp.exp(scores - row_max)
    row_total = jnp.sum(exponent, axis=-1, keepdims=True)
    probability = (exponent / row_total).astype(jnp.bfloat16)
    context = jnp.einsum(
        "shqk,skhd->sqhd", probability, split_heads(values), preferred_element_type=jnp.float32
    )
    return (context.reshape(queries.shape).astype(jnp.bfloat16), row_max + jnp.log(row_total))


def query_side(queries, keys, values, log_total, context_grad):
    scaling = 1.0 / math.sqrt(HD)
    probability = jnp.exp(score_block(queries, keys) - log_total)
    prob_grad = jnp.einsum(
        "sqhd,skhd->shqk",
        split_heads(context_grad),
        split_heads(values),
        preferred_element_type=jnp.float32,
    )
    row_inner = jnp.sum(probability * prob_grad, axis=-1, keepdims=True)
    score_grad = (probability * (prob_grad - row_inner)).astype(jnp.bfloat16)
    query_grad = (
        jnp.einsum(
            "shqk,skhd->sqhd", score_grad, split_heads(keys), preferred_element_type=jnp.float32
        )
        * scaling
    )
    return (probability, score_grad, query_grad.reshape(queries.shape), row_inner)


def pair_terms(probability, score_grad, queries, context_grad, key_shape):
    scaling = 1.0 / math.sqrt(HD)
    key_part = (
        jnp.einsum(
            "shqk,sqhd->skhd", score_grad, split_heads(queries), preferred_element_type=jnp.float32
        )
        * scaling
    )
    value_part = jnp.einsum(
        "shqk,sqhd->skhd",
        probability.astype(jnp.bfloat16),
        split_heads(context_grad),
        preferred_element_type=jnp.float32,
    )
    return (key_part.reshape(key_shape), value_part.reshape(key_shape))


def self_back(queries, keys_all, values_all, log_total, context_grad):
    probability, score_grad, query_grad, row_inner = query_side(
        queries, keys_all, values_all, log_total, context_grad
    )
    key_part, value_part = pair_terms(
        probability, score_grad, queries, context_grad, keys_all.shape
    )
    key_grad, value_grad = (
        lax.psum_scatter(
            key_part.astype(jnp.bfloat16), "seq", scatter_dimension=1, tiled=True
        ).astype(jnp.float32),
        lax.psum_scatter(
            value_part.astype(jnp.bfloat16), "seq", scatter_dimension=1, tiled=True
        ).astype(jnp.float32),
    )
    return (
        query_grad.astype(jnp.bfloat16),
        key_grad.astype(jnp.bfloat16),
        value_grad.astype(jnp.bfloat16),
    )


def on_device(
    layer_input,
    memory,
    timesteps,
    upstream,
    step_table,
    norm_gains,
    shift_rows,
    self_entry,
    self_exit,
    cross_query,
    cross_keyval,
    cross_exit,
    expand_weight,
    expand_bias,
    reduce_weight,
):
    model_width = layer_input.shape[2]
    inputs = layer_input.astype(jnp.float32)
    step_match = (
        timesteps[:, None] == jnp.arange(step_table.shape[0], dtype=jnp.int32)[None, :]
    ).astype(jnp.float32)
    step_rows = jnp.dot(step_match, step_table.astype(jnp.float32), precision=lax.Precision.HIGHEST)
    hidden_one = layer_norm(inputs, norm_gains[0], shift_rows[0]) + step_rows[:, None, :]
    normed_one = hidden_one.astype(jnp.bfloat16)
    entry = project(normed_one, self_entry)
    queries = (entry[..., :model_width] + shift_rows[3]).astype(jnp.bfloat16)
    keys_local = entry[..., model_width : 2 * model_width].astype(jnp.bfloat16)
    values_local = (entry[..., 2 * model_width :] + shift_rows[4]).astype(jnp.bfloat16)
    keys_all, values_all = (
        lax.all_gather(keys_local, "seq", axis=1, tiled=True),
        lax.all_gather(values_local, "seq", axis=1, tiled=True),
    )
    context_one, log_one = attend(queries, keys_all, values_all)
    mixed_one = inputs + project(context_one, self_exit) + shift_rows[5]
    normed_two = layer_norm(mixed_one, norm_gains[1], shift_rows[1]).astype(jnp.bfloat16)
    cross_queries = (project(normed_two, cross_query) + shift_rows[6]).astype(jnp.bfloat16)
    memory_proj = project(memory, cross_keyval)
    memory_keys = memory_proj[..., :model_width].astype(jnp.bfloat16)
    memory_values = (memory_proj[..., model_width:] + shift_rows[7]).astype(jnp.bfloat16)
    keys_far, values_far = (
        lax.all_gather(memory_keys, "seq", axis=1, tiled=True),
        lax.all_gather(memory_values, "seq", axis=1, tiled=True),
    )
    context_two, log_two = attend(cross_queries, keys_far, values_far)
    mixed_two = mixed_one + project(context_two, cross_exit) + shift_rows[8]
    normed_three = layer_norm(mixed_two, norm_gains[2], shift_rows[2]).astype(jnp.bfloat16)
    expanded = project(normed_three, expand_weight) + expand_bias
    activated = gelu_tanh(expanded).astype(jnp.bfloat16)
    result = mixed_two + project(activated, reduce_weight) + shift_rows[9]
    outer_grad = upstream.astype(jnp.float32)
    reduce_grad = weight_grad(activated, upstream)
    final_shift = jnp.sum(outer_grad, axis=(0, 1))
    _, gelu_pull = jax.vjp(gelu_tanh, expanded)
    expanded_grad = gelu_pull(project_back(upstream, reduce_weight))[0].astype(jnp.bfloat16)
    expand_grad = weight_grad(normed_three, expanded_grad)
    expand_bias_grad = column_sums(expanded_grad)
    mixed_two_part, gain_three, shift_three = norm_back(
        mixed_two, norm_gains[2], shift_rows[2], project_back(expanded_grad, expand_weight)
    )
    mixed_two_grad = outer_grad + mixed_two_part
    branch_two = mixed_two_grad.astype(jnp.bfloat16)
    cross_exit_grad = weight_grad(context_two, branch_two)
    cross_out_shift = column_sums(branch_two)
    context_two_grad = project_back(branch_two, cross_exit).astype(jnp.bfloat16)
    probability, score_grad, query_grad, _ = query_side(
        cross_queries, keys_far, values_far, log_two, context_two_grad
    )
    key_part, value_part = pair_terms(
        probability, score_grad, cross_queries, context_two_grad, keys_far.shape
    )
    key_sum, value_sum = (
        lax.psum_scatter(
            key_part.astype(jnp.bfloat16), "seq", scatter_dimension=1, tiled=True
        ).astype(jnp.float32),
        lax.psum_scatter(
            value_part.astype(jnp.bfloat16), "seq", scatter_dimension=1, tiled=True
        ).astype(jnp.float32),
    )
    memory_keys_grad = key_sum.astype(jnp.bfloat16)
    memory_values_grad = value_sum.astype(jnp.bfloat16)
    cross_queries_grad = query_grad.astype(jnp.bfloat16)
    cross_query_grad = weight_grad(normed_two, cross_queries_grad)
    cross_query_shift = column_sums(cross_queries_grad)
    memory_rows_grad = jnp.concatenate([memory_keys_grad, memory_values_grad], axis=-1)
    cross_keyval_grad = weight_grad(memory, memory_rows_grad)
    memory_value_shift = column_sums(memory_values_grad)
    memory_gradient = project_back(memory_rows_grad, cross_keyval)
    mixed_one_part, gain_two, shift_two = norm_back(
        mixed_one, norm_gains[1], shift_rows[1], project_back(cross_queries_grad, cross_query)
    )
    mixed_one_grad = mixed_two_grad + mixed_one_part
    branch_one = mixed_one_grad.astype(jnp.bfloat16)
    self_exit_grad = weight_grad(context_one, branch_one)
    self_out_shift = column_sums(branch_one)
    context_one_grad = project_back(branch_one, self_exit).astype(jnp.bfloat16)
    queries_grad, keys_grad, values_grad = self_back(
        queries, keys_all, values_all, log_one, context_one_grad
    )
    entry_rows_grad = jnp.concatenate([queries_grad, keys_grad, values_grad], axis=-1)
    entry_grad = weight_grad(normed_one, entry_rows_grad)
    query_shift = column_sums(queries_grad)
    value_shift = column_sums(values_grad)
    hidden_one_grad = project_back(entry_rows_grad, self_entry)
    table_grad = jnp.dot(
        step_match.T, jnp.sum(hidden_one_grad, axis=1), precision=lax.Precision.HIGHEST
    )
    input_part, gain_one, shift_one = norm_back(
        inputs, norm_gains[0], shift_rows[0], hidden_one_grad
    )
    input_gradient = mixed_one_grad + input_part
    gains_grad = jnp.stack([gain_one, gain_two, gain_three])
    shifts_grad = jnp.stack(
        [
            shift_one,
            shift_two,
            shift_three,
            query_shift,
            value_shift,
            self_out_shift,
            cross_query_shift,
            memory_value_shift,
            cross_out_shift,
            final_shift,
        ]
    )
    (
        table_sum,
        gains_sum,
        shifts_sum,
        entry_sum,
        self_exit_sum,
        cross_query_sum,
        cross_keyval_sum,
        cross_exit_sum,
        expand_sum,
        expand_bias_sum,
        reduce_sum,
    ) = lax.psum(
        (
            table_grad,
            gains_grad,
            shifts_grad,
            entry_grad,
            self_exit_grad,
            cross_query_grad,
            cross_keyval_grad,
            cross_exit_grad,
            expand_grad,
            expand_bias_grad,
            reduce_grad,
        ),
        ("dp", "seq"),
    )
    return (
        result,
        input_gradient,
        memory_gradient,
        table_sum,
        gains_sum,
        shifts_sum,
        entry_sum,
        self_exit_sum,
        cross_query_sum,
        cross_keyval_sum,
        cross_exit_sum,
        expand_sum,
        expand_bias_sum,
        reduce_sum,
    )


def solution(mesh):
    placed = (
        P("dp", "seq", None),
        P("dp", "seq", None),
        P("dp"),
        P("dp", "seq", None),
        P(),
        P(),
        P(),
        P(),
        P(),
        P(),
        P(),
        P(),
        P(),
        P(),
        P(),
    )
    return jax.shard_map(
        on_device,
        mesh=mesh,
        in_specs=placed,
        out_specs=(
            P("dp", "seq", None),
            P("dp", "seq", None),
            P("dp", "seq", None),
            P(),
            P(),
            P(),
            P(),
            P(),
            P(),
            P(),
            P(),
            P(),
            P(),
            P(),
        ),
        check_vma=False,
    )
```

profile of v0, /device:TPU:0, one launch (start us, length us, event | category | flops | bytes accessed | tf_op | source)
XLA Modules:
  0.0 625.2 jit_solution(8532991732260900189)
XLA Ops:
  28.6 15.5 %all-gather.7.cloned.1.call-done = bf16[2,1024,512]{2,1,0:T(8,128)(2,1)} async-done(((bf16[2,256,512]{2,1,0:T(8,128)(2,1)}), bf16[2,1024,512]{2,1,0:T(8,128)(2,1)}) %all-gather.7.cloned.1.call-update) | async-done | bytes 2097168 | tf_op jit(solution)/shard_map/all_gather | solution.py:164
  48.0 4.1 multiply_reduce_fusion.3
  52.1 6.1 copy-done.1
  61.8 7.1 %all-gather.5.cloned.1.call-done = bf16[2,1024,512]{2,1,0:T(8,128)(2,1)} async-done(((bf16[2,256,512]{2,1,0:T(8,128)(2,1)}), bf16[2,1024,512]{2,1,0:T(8,128)(2,1)}) %all-gather.5.cloned.1.call-update) | async-done | bytes 2097168 | tf_op jit(solution)/shard_map/all_gather | solution.py:165
  72.8 9.3 %fusion.54 = bf16[2,8,64,256]{3,2,1,0:T(8,128)(2,1)S(1)} fusion(bf16[2,1024,8,64]{1,3,2,0:T(8,128)(2,1)} %bitcast.167, f32[2,8,256,1024]{3,2,1,0:T(8,128)} %copy-done.1, f32[2,8,256]{2,1,0:T(8,128)S(1)} %fusion, f32[2,8,256]{2,1,0:T(8,128)S(1)} %get-tuple-element.87), kind=kOutput, calls=%fused_computation.84 | convolution fusion | flops 553910272 | bytes 19431424 | tf_op jit(solution)/shard_map/shqk,skhd->sqhd/dot_general | solution.py:69
  86.5 7.1 %all-gather.11.cloned.1.call-done = bf16[2,1024,512]{2,1,0:T(8,128)(2,1)} async-done(((bf16[2,256,512]{2,1,0:T(8,128)(2,1)}), bf16[2,1024,512]{2,1,0:T(8,128)(2,1)}) %all-gather.11.cloned.1.call-update) | async-done | bytes 2097168 | tf_op jit(solution)/shard_map/all_gather | solution.py:175
  97.5 4.2 multiply_reduce_fusion.2
  107.8 10.3 %all-gather.9.cloned.1.call-done = bf16[2,1024,512]{2,1,0:T(8,128)(2,1)} async-done(((bf16[2,256,512]{2,1,0:T(8,128)(2,1)}), bf16[2,1024,512]{2,1,0:T(8,128)(2,1)}) %all-gather.9.cloned.1.call-update) | async-done | bytes 2097168 | tf_op jit(solution)/shard_map/all_gather | solution.py:176
  122.1 8.6 %fusion.53 = bf16[2,8,64,256]{3,2,1,0:T(8,128)(2,1)S(1)} fusion(bf16[2,1024,8,64]{1,3,2,0:T(8,128)(2,1)} %bitcast.169, f32[2,8,256,1024]{3,2,1,0:T(8,128)} %copy-done.2, f32[2,8,256]{2,1,0:T(8,128)S(1)} %fusion.1, f32[2,8,256]{2,1,0:T(8,128)S(1)} %get-tuple-element.91), kind=kOutput, calls=%fused_computation.83 | convolution fusion | flops 553910272 | bytes 19431424 | tf_op jit(solution)/shard_map/shqk,skhd->sqhd/dot_general | solution.py:69
  145.5 12.3 %multiply_reduce_fusion.1 = (f32[2,8,256]{2,1,0:T(8,128)S(1)}, f32[2,8,256,1024]{3,2,1,0:T(8,128)}) fusion(f32[2,8,256,1024]{3,2,1,0:T(8,128)} %copy-done.2, f32[2,8,256]{2,1,0:T(8,128)S(1)} %log_add_fusion.1, bf16[2,256,8,64]{1,3,2,0:T(8,128)(2,1)} %bitcast.177, bf16[2,1024,8,64]{1,3,2,0:T(8,128)(2,1)} %bitcast.170), kind=kOutput, calls=%fused_computation.4 | convolution fusion | flops 553644032 | bytes 36208640 | tf_op jit(solution)/shard_map/sqhd,skhd->shqk/dot_general | solution.py:78
  157.8 12.3 %multiply_convert_fusion.1 = bf16[2,8,256,1024]{3,2,1,0:T(8,128)(2,1)S(1)} fusion(f32[2,8,256,1024]{3,2,1,0:T(8,128)} %get-tuple-element.97, f32[2,8,256,1024]{3,2,1,0:T(8,128)} %copy-done.2, f32[2,8,256]{2,1,0:T(8,128)S(1)} %get-tuple-element.96, f32[2,8,256]{2,1,0:T(8,128)S(1)} %log_add_fusion.1), kind=kLoop, calls=%fused_computation.3 | loop fusion | flops 20971520 | bytes 41975808 | tf_op jit(solution)/shard_map/convert_element_type | solution.py:85
  174.0 4.0 copy.74
  178.1 10.7 %fusion.28 = bf16[2,8,64,1024]{3,2,1,0:T(8,128)(2,1)} fusion(bf16[2,256,8,64]{1,3,2,0:T(8,128)(2,1)} %bitcast.178, f32[2,8,256,1024]{3,2,1,0:T(8,128)} %copy-done.2, f32[2,8,256]{2,1,0:T(8,128)S(1)} %log_add_fusion.1), kind=kOutput, calls=%fused_computation.47 | convolution fusion | flops 550502400 | bytes 19415040 | tf_op jit(solution)/shard_map/shqk,sqhd->skhd/dot_general | solution.py:103
  192.8 7.2 %convert_reduce_fusion.5 = (f32[8,64]{1,0:T(8,128)S(1)}, bf16[2,8,64,256]{3,2,1,0:T(8,128)(2,1)S(1)}) fusion(bf16[2,1024,8,64]{1,3,2,0:T(8,128)(2,1)} %bitcast.164, bf16[2,8,256,1024]{3,2,1,0:T(8,128)(2,1)} %copy-done.3), kind=kOutput, calls=%fused_computation.107 | convolution fusion | flops 537918976 | bytes 11012096 | tf_op jit(solution)/shard_map/shqk,skhd->sqhd/dot_general | solution.py:87
  206.4 10.4 %fusion.31 = bf16[2,8,64,1024]{3,2,1,0:T(8,128)(2,1)} fusion(bf16[2,256,8,64]{1,3,2,0:T(8,128)(2,1)} %bitcast.179, f32[2,8,256,1024]{3,2,1,0:T(8,128)} %copy-done.1, f32[2,8,256]{2,1,0:T(8,128)S(1)} %log_add_fusion), kind=kOutput, calls=%fused_computation.48 | convolution fusion | flops 550502400 | bytes 19415040 | tf_op jit(solution)/shard_map/shqk,sqhd->skhd/dot_general | solution.py:103
  216.8 4.1 copy.72
  221.0 12.5 %multiply_reduce_fusion = (f32[2,8,256]{2,1,0:T(8,128)S(1)}, f32[2,8,256,1024]{3,2,1,0:T(8,128)}) fusion(f32[2,8,256,1024]{3,2,1,0:T(8,128)} %copy-done.1, f32[2,8,256]{2,1,0:T(8,128)S(1)} %log_add_fusion, bf16[2,256,8,64]{1,3,2,0:T(8,128)(2,1)} %bitcast.180, bf16[2,1024,8,64]{1,3,2,0:T(8,128)(2,1)} %bitcast.168), kind=kOutput, calls=%fused_computation.1 | convolution fusion | flops 553644032 | bytes 36208640 | tf_op jit(solution)/shard_map/sqhd,skhd->shqk/dot_general | solution.py:78
  233.5 12.1 %multiply_convert_fusion = bf16[2,8,256,1024]{3,2,1,0:T(8,128)(2,1)S(1)} fusion(f32[2,8,256,1024]{3,2,1,0:T(8,128)} %get-tuple-element.100, f32[2,8,256,1024]{3,2,1,0:T(8,128)} %copy-done.1, f32[2,8,256]{2,1,0:T(8,128)S(1)} %get-tuple-element.99, f32[2,8,256]{2,1,0:T(8,128)S(1)} %log_add_fusion), kind=kLoop, calls=%fused_computation | loop fusion | flops 20971520 | bytes 41975808 | tf_op jit(solution)/shard_map/convert_element_type | solution.py:85
  253.6 7.6 %convert_reduce_fusion.8 = (f32[8,64]{1,0:T(8,128)S(1)}, bf16[2,8,64,256]{3,2,1,0:T(8,128)(2,1)}) fusion(bf16[2,1024,8,64]{1,3,2,0:T(8,128)(2,1)} %bitcast.162, bf16[2,8,256,1024]{3,2,1,0:T(8,128)(2,1)} %copy-done.4), kind=kOutput, calls=%fused_computation.110 | convolution fusion | flops 537918976 | bytes 11012096 | tf_op jit(solution)/shard_map/shqk,skhd->sqhd/dot_general | solution.py:87
  274.2 4.0 convolution_bitcast_fusion
  285.3 25.0 %reduce-scatter.5.cloned.1.call-done = bf16[2,256,512]{2,1,0:T(8,128)(2,1)} async-done(((bf16[2,1024,512]{2,1,0:T(8,128)(2,1)}), bf16[2,256,512]{2,1,0:T(8,128)(2,1)}) %reduce-scatter.5.cloned.1.call-update) | async-done | bytes 524304 | tf_op jit(solution)/shard_map/reduce_scatter | solution.py:120
  319.4 4.9 fusion.47
  327.0 42.5 %all-reduce = (f32[3,512]{1,0:T(4,128)}, f32[10,512]{1,0:T(8,128)}, f32[2048]{0:T(1024)}) all-reduce(f32[3,512]{1,0:T(4,128)S(1)} %pad_maximum_fusion.3, f32[10,512]{1,0:T(8,128)S(1)} %stack.59, f32[2048]{0:T(1024)S(1)} %get-tuple-element.106), channel_id=1, replica_groups=mesh['dp'=8,'seq'=4] {'dp','seq'}, use_global_device_ids=true, to_apply=%region_27.0 | all-reduce | flops 8704 | bytes 69632 | tf_op jit(solution)/shard_map/psum | solution.py:272
  375.3 226.8 %all-reduce.4.cloned.1.call-done = (f32[50,512]{1,0:T(8,128)}, f32[512,1536]{1,0:T(8,128)}, f32[512,512]{1,0:T(8,128)}, f32[512,512]{1,0:T(8,128)}, f32[512,1024...) async-done(((f32[50,512]{1,0:T(8,128)}, f32[512,1536]{1,0:T(8,128)}, f32[512,512]{1,0:T(8,128)}, f32[512,512]{1,0:T(8,128)}, ...) | async-done | bytes 16879632 | tf_op jit(solution)/shard_map/psum | solution.py:272
  (234 shorter events, 141.6 us)
Async XLA Ops:
  7.2 127.1 %copy-start = (bf16[2048,512]{1,0:T(8,128)(2,1)S(1)}, bf16[2048,512]{1,0:T(8,128)(2,1)}, u32[]{:S(2)}) copy-start(bf16[2048,512]{1,0:T(8,128)(2,1)} %param.29) | copy-start | bytes 6291460
  7.2 36.9 %all-gather.7.cloned.1.call-start = ((), (), s32[]{:S(2)}) async-start(), calls=%async_computation.5 | async-start | bytes 2621440 | tf_op jit(solution)/shard_map/all_gather | solution.py:164
  8.6 12.8 %copy-start.50 = (f32[2,256]{1,0:T(2,128)}, f32[2,256]{1,0:T(2,128)S(1)}, u32[]{:S(2)}) copy-start(f32[2,256]{1,0:T(2,128)S(1)} %broadcast_multiply_fusion.2) | copy-start | bytes 6148
  9.9 11.4 %copy-start.52 = (f32[2,256]{1,0:T(2,128)}, f32[2,256]{1,0:T(2,128)S(1)}, u32[]{:S(2)}) copy-start(f32[2,256]{1,0:T(2,128)S(1)} %fusion.82) | copy-start | bytes 6148
  18.7 50.2 %all-gather.5.cloned.1.call-start = ((), (), s32[]{:S(2)}) async-start(), calls=%async_computation.4 | async-start | bytes 2621440 | tf_op jit(solution)/shard_map/all_gather | solution.py:165
  21.4 72.2 %all-gather.11.cloned.1.call-start = ((), (), s32[]{:S(2)}) async-start(), calls=%async_computation.7 | async-start | bytes 2621440 | tf_op jit(solution)/shard_map/all_gather | solution.py:175
  25.6 92.6 %all-gather.9.cloned.1.call-start = ((), (), s32[]{:S(2)}) async-start(), calls=%async_computation.6 | async-start | bytes 2621440 | tf_op jit(solution)/shard_map/all_gather | solution.py:176
  27.8 250.4 %reduce-scatter.9.cloned.1.call-start = ((), (), s32[]{:S(2)}) async-start(), calls=%async_computation.10 | async-start | bytes 2621440 | tf_op jit(solution)/shard_map/reduce_scatter | solution.py:206
  28.6 23.5 %copy-start.14 = (bf16[2,256,512]{1,2,0:T(8,128)(2,1)}, bf16[2,256,512]{1,2,0:T(8,128)(2,1)S(1)}, u32[]{:S(2)}) copy-start(bf16[2,256,512]{1,2,0:T(8,128)(2,1)S(1)} %copy.61) | copy-start | bytes 1572868
  157.8 12.3 %copy-start.16 = (bf16[2,256,512]{1,2,0:T(8,128)(2,1)S(1)}, bf16[2,256,512]{1,2,0:T(8,128)(2,1)}, u32[]{:S(2)}) copy-start(bf16[2,256,512]{1,2,0:T(8,128)(2,1)} %copy.65) | copy-start | bytes 1572868
  178.0 102.1 %reduce-scatter.11.cloned.1.call-start = ((), (), s32[]{:S(2)}) async-start(), calls=%async_computation.11 | async-start | bytes 2621440 | tf_op jit(solution)/shard_map/reduce_scatter | solution.py:209
  192.7 92.6 %reduce-scatter.7.cloned.1.call-start = ((), (), s32[]{:S(2)}) async-start(), calls=%async_computation.9 | async-start | bytes 2621440 | tf_op jit(solution)/shard_map/reduce_scatter | solution.py:123
  220.9 89.4 %reduce-scatter.5.cloned.1.call-start = ((), (), s32[]{:S(2)}) async-start(), calls=%async_computation.8 | async-start | bytes 2621440 | tf_op jit(solution)/shard_map/reduce_scatter | solution.py:120
  233.5 12.1 %copy-start.15 = (bf16[2,256,512]{1,2,0:T(8,128)(2,1)S(1)}, bf16[2,256,512]{1,2,0:T(8,128)(2,1)}, u32[]{:S(2)}) copy-start(bf16[2,256,512]{1,2,0:T(8,128)(2,1)} %copy-done.14) | copy-start | bytes 1572868
  253.6 348.6 %all-reduce.4.cloned.1.call-start = ((), (), s32[]{:S(2)}) async-start(), calls=%async_computation.12 | async-start | bytes 33783808 | tf_op jit(solution)/shard_map/psum | solution.py:272
  278.2 32.2 %copy-start.11 = (bf16[2,256,512]{2,1,0:T(8,128)(2,1)S(1)}, bf16[2,256,512]{2,1,0:T(8,128)(2,1)}, u32[]{:S(2)}) copy-start(bf16[2,256,512]{2,1,0:T(8,128)(2,1)} %param.15) | copy-start | bytes 1572868
  278.2 32.2 %copy-start.51 = (f32[2,256]{1,0:T(2,128)S(1)}, f32[2,256]{1,0:T(2,128)}, u32[]{:S(2)}) copy-start(f32[2,256]{1,0:T(2,128)} %copy-done.50) | copy-start | bytes 6148
  278.2 32.2 %copy-start.55 = (f32[1,512]{1,0:T(1,128)S(1)}, f32[1,512]{1,0:T(1,128)}, u32[]{:S(2)}) copy-start(f32[1,512]{1,0:T(1,128)} %copy-done.54) | copy-start | bytes 6148
  285.3 29.1 %copy-start.61 = (s32[2]{0:T(128)S(1)}, s32[2]{0:T(128)}, u32[]{:S(2)}) copy-start(s32[2]{0:T(128)} %param.17) | copy-start | bytes 28
  285.3 30.1 %copy-start.53 = (f32[2,256]{1,0:T(2,128)S(1)}, f32[2,256]{1,0:T(2,128)}, u32[]{:S(2)}) copy-start(f32[2,256]{1,0:T(2,128)} %copy-done.52) | copy-start | bytes 6148
  285.3 30.1 %copy-start.60 = (f32[1,512]{1,0:T(1,128)S(1)}, f32[1,512]{1,0:T(1,128)}, u32[]{:S(2)}) copy-start(f32[1,512]{1,0:T(1,128)} %copy-done.59) | copy-start | bytes 6148
  285.3 30.1 %copy-start.65 = (f32[2,512]{1,0:T(2,128)S(1)}, f32[2,512]{1,0:T(2,128)}, u32[]{:S(2)}) copy-start(f32[2,512]{1,0:T(2,128)} %copy-done.64) | copy-start | bytes 12292
  285.3 30.0 %copy-start.44 = (bf16[2,256,512]{2,1,0:T(8,128)(2,1)S(1)}, bf16[2,256,512]{2,1,0:T(8,128)(2,1)}, u32[]{:S(2)}) copy-start(bf16[2,256,512]{2,1,0:T(8,128)(2,1)} %reduce-scatter.7.cloned.1.call-done) | copy-start | bytes 1572868
  324.3 48.5 %copy-start.9 = (f32[2,256,512]{2,1,0:T(8,128)S(1)}, f32[2,256,512]{2,1,0:T(8,128)}, u32[]{:S(2)}) copy-start(f32[2,256,512]{2,1,0:T(8,128)} %copy-done.8) | copy-start | bytes 3145732
  (51 other events, 234.7 us)
Sparse Core Ops, SparseCore 0:
  18.8 25.2 all-gather.6
  46.3 22.5 all-gather.4
  71.0 22.5 all-gather.10
  95.6 22.5 all-gather.8
  178.2 31.1 reduce-scatter.8
  211.7 31.1 reduce-scatter.10
  245.5 31.1 reduce-scatter.6
  279.2 31.1 reduce-scatter.4
  318.3 283.7 all-reduce.3
where the time goes:
time: 630 us; the launch traced here: 625 us
  waiting for transfers between devices  292 us (46%)
  matrix products  146 us (23%)
  local copies, waits for them, and re-layouts  82.7 us (13%)
  other arithmetic  46.4 us (7%)
  blocking collectives  42.5 us (7%)
  between operations  14.7 us (2%)
    psum x1, waiting for transfers between devices, on_device(): lax.psum((table_grad, gains_grad, shifts_grad, entry_grad, self_exit_grad...  227 us
    psum x1, blocking collectives, on_device(): lax.psum((table_grad, gains_grad, shifts_grad, entry_grad, self_exit_grad...  42.5 us
    unnamed x141, local copies, waits for them, and re-layouts  36.3 us
    reduce_scatter x1, waiting for transfers between devices, self_back(): lax.psum_scatter(key_part.astype(jnp.bfloat16), 'seq', scatter_dimension=...  25 us
    dot_general x2, matrix products, query_side(): jnp.einsum('sqhd,skhd->shqk', split_heads(context_grad), split_heads(valu...  24.9 us
    convert_element_type x2, other arithmetic, query_side(): score_grad = (probability * (prob_grad - row_inner)).astype(jnp.bfloat16)  24.4 us
    dot_general x2, matrix products, pair_terms(): jnp.einsum('shqk,sqhd->skhd', probability.astype(jnp.bfloat16), split_hea...  21.1 us
    dot_general x7, matrix products, weight_grad(): jnp.einsum('sqd,sqe->de', row_block, grad_block, preferred_element_type=j...  20.9 us
  transfers between devices with their start and end apart: 9, of which 6 were waited for; matrix products, arithmetic and copies ran while one was open for 27% of the time, Pallas kernels for 0%

commit v1 on v0

v1 whole, which is shorter than its diff:
```python
import functools
import math

import jax
import jax.numpy as jnp
from jax import lax
from jax.experimental import pallas as pl
from jax.experimental.pallas import tpu as pltpu
from jax.sharding import PartitionSpec as P

HD = 64
PAIR = 2 * HD
EPSILON = 1e-05
SCALING = 1.0 / math.sqrt(HD)
BF = jnp.bfloat16
F32 = jnp.float32
NT = (((1,), (1,)), ((), ()))
NN = (((1,), (0,)), ((), ()))
TN = (((0,), (0,)), ((), ()))


def dot(left, right, dims=NN):
    return lax.dot_general(left, right, dims, preferred_element_type=F32)


def norm_parts(values):
    centered = values - jnp.mean(values, axis=-1, keepdims=True)
    inverse = lax.rsqrt(jnp.mean(centered * centered, axis=-1, keepdims=True) + EPSILON)
    return centered * inverse, inverse


def norm_back(values, gain, incoming):
    unit, inverse = norm_parts(values)
    scaled = incoming * gain
    grad = inverse * (
        scaled
        - jnp.mean(scaled, axis=-1, keepdims=True)
        - unit * jnp.mean(scaled * unit, axis=-1, keepdims=True)
    )
    return grad, jnp.sum(incoming * unit, axis=0), jnp.sum(incoming, axis=0)


def column_sums(rows):
    return jnp.sum(rows.astype(F32), axis=0)


def attend_body(q_ref, k_ref, v_ref, o_ref, l_ref):
    lane = lax.broadcasted_iota(jnp.int32, (1, PAIR), 1)
    sub = lax.broadcasted_iota(jnp.int32, (PAIR, 1), 0)
    keys = k_ref[...]
    values = v_ref[...].T
    values = jnp.concatenate([values, jnp.ones((16, values.shape[1]), BF)], axis=0)
    queries = q_ref[...]
    outs = []
    for head in range(2):
        mine = (lane < HD) if head == 0 else (lane >= HD)
        scores = dot(keys, jnp.where(mine, queries, jnp.zeros_like(queries)), NT)
        top = jnp.max(scores, axis=0, keepdims=True)
        weight = jnp.exp(scores - top).astype(BF)
        summed = dot(values, weight)
        total = summed[PAIR : PAIR + 1]
        outs.append(summed[:PAIR] / total)
        l_ref[0, head : head + 1, :] = top + jnp.log(total)
    o_ref[...] = jnp.where(sub < HD, outs[0], outs[1]).T.astype(BF)


def attend(queries, keys, values):
    nq, width = queries.shape
    nk = keys.shape[0]
    pairs = width // PAIR
    row = lambda n: pl.BlockSpec((n, PAIR), lambda j: (0, j))
    return pl.pallas_call(
        attend_body,
        grid=(pairs,),
        in_specs=[row(nq), row(nk), row(nk)],
        out_specs=[row(nq), pl.BlockSpec((1, 2, nq), lambda j: (j, 0, 0))],
        out_shape=[
            jax.ShapeDtypeStruct((nq, width), BF),
            jax.ShapeDtypeStruct((pairs, 2, nq), F32),
        ],
        cost_estimate=pl.CostEstimate(
            flops=16 * nq * nk * width, bytes_accessed=4 * (nq + nk) * width, transcendentals=0
        ),
        name="attend",
    )(queries, keys, values)


def attend_back_body(tile, q_ref, k_ref, v_ref, o_ref, c_ref, l_ref, dq_ref, dk_ref, dv_ref):
    lane = lax.broadcasted_iota(jnp.int32, (1, PAIR), 1)
    sub = lax.broadcasted_iota(jnp.int32, (PAIR, 1), 0)
    queries = q_ref[...]
    incoming = c_ref[...]
    product = (incoming.astype(F32) * o_ref[...].astype(F32)).T
    inner = [
        jnp.sum(product[:HD], axis=0, keepdims=True),
        jnp.sum(product[HD:], axis=0, keepdims=True),
    ]
    one_q, one_c = [], []
    for head in range(2):
        mine = (lane < HD) if head == 0 else (lane >= HD)
        one_q.append(jnp.where(mine, queries, jnp.zeros_like(queries)))
        one_c.append(jnp.where(mine, incoming, jnp.zeros_like(incoming)))
    dq = [None, None]
    for start in range(0, k_ref.shape[0], tile):
        keys = k_ref[start : start + tile, :]
        values = v_ref[start : start + tile, :]
        turned = keys.T
        dk, dv = [], []
        for head in range(2):
            scores = dot(keys, one_q[head], NT)
            prob = jnp.exp(scores - l_ref[0, head : head + 1, :])
            prob_grad = dot(values, one_c[head], NT)
            score_grad = (prob * (prob_grad - inner[head])).astype(BF)
            dv.append(dot(prob.astype(BF), incoming))
            dk.append(dot(score_grad, queries))
            part = dot(turned, score_grad)
            dq[head] = part if dq[head] is None else dq[head] + part
        dk_ref[start : start + tile, :] = jnp.where(lane < HD, dk[0], dk[1]).astype(BF)
        dv_ref[start : start + tile, :] = jnp.where(lane < HD, dv[0], dv[1]).astype(BF)
    dq_ref[...] = (jnp.where(sub < HD, dq[0], dq[1]) * SCALING).T.astype(BF)


def attend_back(queries, keys, values, context, incoming, log_total):
    nq, width = queries.shape
    nk = keys.shape[0]
    pairs = width // PAIR
    row = lambda n: pl.BlockSpec((n, PAIR), lambda j: (0, j))
    return pl.pallas_call(
        functools.partial(attend_back_body, nk // 2),
        grid=(pairs,),
        in_specs=[
            row(nq),
            row(nk),
            row(nk),
            row(nq),
            row(nq),
            pl.BlockSpec((1, 2, nq), lambda j: (j, 0, 0)),
        ],
        out_specs=[row(nq), row(nk), row(nk)],
        out_shape=[
            jax.ShapeDtypeStruct((nq, width), BF),
            jax.ShapeDtypeStruct((nk, width), BF),
            jax.ShapeDtypeStruct((nk, width), BF),
        ],
        cost_estimate=pl.CostEstimate(
            flops=40 * nq * nk * width, bytes_accessed=6 * (nq + nk) * width, transcendentals=0
        ),
        name="attend_back",
    )(queries, keys, values, context, incoming, log_total)


def swap(value, axis, size, bit):
    return lax.ppermute(value, axis, [(i, i ^ (1 << bit)) for i in range(size)])


def rank_bit(axis, bit):
    return (lax.axis_index(axis) >> bit) & 1


def to_segments(value, chips):
    y = lax.axis_index("seq") // 2
    blocks = [lax.dynamic_index_in_dim(value, y, 0, keepdims=False)]
    for k in range(1, chips):
        out = lax.dynamic_index_in_dim(value, (y + k) % chips, 0, keepdims=False)
        pairs = [(i, (i + 2 * k) % (2 * chips)) for i in range(2 * chips)]
        blocks.append(lax.ppermute(out, "seq", pairs))
    return jnp.concatenate(blocks, axis=0)


def from_segments(value, chips, dtype=BF):
    y = lax.axis_index("seq") // 2
    rows = value.shape[0] // chips
    whole = jnp.zeros((chips, rows, value.shape[1]), F32)
    whole = lax.dynamic_update_index_in_dim(whole, value[:rows], y, 0)
    for k in range(1, chips):
        out = value[k * rows : (k + 1) * rows].astype(dtype)
        pairs = [(i, (i - 2 * k) % (2 * chips)) for i in range(2 * chips)]
        got = lax.ppermute(out, "seq", pairs).astype(F32)
        whole = lax.dynamic_update_index_in_dim(whole, got, (y + k) % chips, 0)
    return whole


def reduce_all(stack, bits, sizes):
    rows = stack.shape[1]
    levels = min(len(bits), int(math.log2(rows // 16)))
    value = stack
    for axis, bit in bits[:levels]:
        half = value.shape[1] // 2
        mine = rank_bit(axis, bit)
        away = lax.dynamic_slice_in_dim(value, (1 - mine) * half, half, 1)
        got = swap(away, axis, sizes[axis], bit)
        value = lax.dynamic_slice_in_dim(value, mine * half, half, 1)
        value = (value.astype(F32) + got.astype(F32)).astype(BF)
    for axis, bit in bits[levels:]:
        got = swap(value, axis, sizes[axis], bit)
        value = (value.astype(F32) + got.astype(F32)).astype(BF)
    for axis, bit in reversed(bits[:levels]):
        got = swap(value, axis, sizes[axis], bit)
        mine = rank_bit(axis, bit)
        value = jnp.where(
            mine == 0,
            jnp.concatenate([value, got], axis=1),
            jnp.concatenate([got, value], axis=1),
        )
    return value


def sum_all(value, bits, sizes):
    for axis, bit in bits:
        value = value + swap(value, axis, sizes[axis], bit)
    return value


def on_device(
    sizes,
    layer_input,
    memory,
    timesteps,
    upstream,
    step_table,
    norm_gains,
    shift_rows,
    self_entry,
    self_exit,
    cross_query,
    cross_keyval,
    cross_exit,
    expand_weight,
    expand_bias,
    reduce_weight,
):
    chips = sizes["seq"] // 2
    d = layer_input.shape[2]
    dp_bits = [("dp", b) for b in range(sizes["dp"].bit_length() - 1)]
    seq_bits = [("seq", b) for b in range(sizes["seq"].bit_length() - 1)]
    order_a = [seq_bits[0], dp_bits[0]] + seq_bits[1:] + dp_bits[1:]
    order_b = seq_bits + dp_bits

    x_own = to_segments(layer_input, chips)
    x_oth = swap(x_own, "seq", sizes["seq"], 0)
    m_own = to_segments(memory, chips)
    m_oth = swap(m_own, "seq", sizes["seq"], 0)
    up = to_segments(upstream, chips)
    step = lax.dynamic_index_in_dim(timesteps, lax.axis_index("seq") // 2, 0, keepdims=False)
    step_row = lax.dynamic_index_in_dim(step_table, step, 0).astype(F32)

    own = x_own.shape[0]
    x_all = jnp.concatenate([x_own, x_oth], axis=0)
    m_all = jnp.concatenate([m_own, m_oth], axis=0)
    inputs = x_all.astype(F32)
    unit, _ = norm_parts(inputs)
    normed_one = (unit * norm_gains[0] + shift_rows[0] + step_row).astype(BF)
    queries = (dot(normed_one[:own], self_entry[:, :d]) + shift_rows[3]).astype(BF) * BF(SCALING)
    keyval = dot(normed_one, self_entry[:, d:])
    keys = keyval[:, :d].astype(BF)
    values = (keyval[:, d:] + shift_rows[4]).astype(BF)
    context_one, log_one = attend(queries, keys, values)
    mixed_one = inputs[:own] + dot(context_one, self_exit) + shift_rows[5]
    unit, _ = norm_parts(mixed_one)
    normed_two = (unit * norm_gains[1] + shift_rows[1]).astype(BF)
    far_queries = (dot(normed_two, cross_query) + shift_rows[6]).astype(BF) * BF(SCALING)
    far = dot(m_all, cross_keyval)
    far_keys = far[:, :d].astype(BF)
    far_values = (far[:, d:] + shift_rows[7]).astype(BF)
    context_two, log_two = attend(far_queries, far_keys, far_values)
    mixed_two = mixed_one + dot(context_two, cross_exit) + shift_rows[8]
    unit, _ = norm_parts(mixed_two)
    normed_three = (unit * norm_gains[2] + shift_rows[2]).astype(BF)
    expanded = dot(normed_three, expand_weight) + expand_bias
    gelu = lambda u: jax.nn.gelu(u, approximate=True)
    activated, gelu_pull = jax.vjp(gelu, expanded)
    activated = activated.astype(BF)
    result = mixed_two + dot(activated, reduce_weight) + shift_rows[9]
    result = from_segments(result, chips)

    stacked = lambda left, right: jnp.stack(
        [dot(left, right[:, i : i + d], TN).astype(BF) for i in range(0, right.shape[1], d)]
    )
    reduce_grad = dot(activated, up, TN).astype(BF).reshape(-1, d, d)
    expanded_grad = gelu_pull(dot(up, reduce_weight, NT))[0].astype(BF)
    expand_grad = stacked(normed_three, expanded_grad)
    reduce_sum = reduce_all(reduce_grad, order_a, sizes)
    expand_sum = reduce_all(expand_grad, order_b, sizes)
    expand_bias_grad = column_sums(expanded_grad).reshape(-1, d)
    part, gain_three, shift_three = norm_back(
        mixed_two, norm_gains[2], dot(expanded_grad, expand_weight, NT)
    )
    mixed_two_grad = up.astype(F32) + part
    branch_two = mixed_two_grad.astype(BF)
    context_two_grad = dot(branch_two, cross_exit, NT).astype(BF)
    dq, dk, dv = attend_back(
        far_queries, far_keys, far_values, context_two, context_two_grad, log_two
    )
    cross_grads = jnp.stack(
        [
            dot(context_two, branch_two, TN).astype(BF),
            dot(normed_two, dq, TN).astype(BF),
            dot(m_all, dk, TN).astype(BF),
            dot(m_all, dv, TN).astype(BF),
        ]
    )
    cross_sum = reduce_all(cross_grads, order_a, sizes)
    far_query_shift = column_sums(dq)
    far_value_shift = column_sums(dv)
    memory_part = dot(dk, cross_keyval[:, :d], NT) + dot(dv, cross_keyval[:, d:], NT)
    got = swap(memory_part[own:].astype(BF), "seq", sizes["seq"], 0)
    memory_gradient = from_segments(memory_part[:own] + got.astype(F32), chips)

    part, gain_two, shift_two = norm_back(
        mixed_one, norm_gains[1], dot(dq, cross_query, NT)
    )
    mixed_one_grad = mixed_two_grad + part
    branch_one = mixed_one_grad.astype(BF)
    context_one_grad = dot(branch_one, self_exit, NT).astype(BF)
    dq, dk, dv = attend_back(queries, keys, values, context_one, context_one_grad, log_one)
    entry_grads = jnp.stack(
        [
            dot(context_one, branch_one, TN).astype(BF),
            dot(normed_one[:own], dq, TN).astype(BF),
            dot(normed_one, dk, TN).astype(BF),
            dot(normed_one, dv, TN).astype(BF),
        ]
    )
    entry_sum = reduce_all(entry_grads, order_b, sizes)
    hidden = dot(dk, self_entry[:, d : 2 * d], NT) + dot(dv, self_entry[:, 2 * d :], NT)
    hidden = hidden + jnp.concatenate(
        [dot(dq, self_entry[:, :d], NT), jnp.zeros((hidden.shape[0] - own, d), F32)]
    )
    part, gain_one, shift_one = norm_back(inputs, norm_gains[0], hidden)
    got = swap(part[own:].astype(BF), "seq", sizes["seq"], 0)
    input_gradient = from_segments(mixed_one_grad + part[:own] + got.astype(F32), chips)

    steps = step_table.shape[0]
    match = (jnp.arange(steps, dtype=jnp.int32) == step).astype(F32)
    table_grad = match[:, None] * jnp.sum(hidden, axis=0)[None, :]
    rows = [
        gain_one,
        gain_two,
        gain_three,
        shift_one,
        shift_two,
        shift_three,
        column_sums(dq),
        column_sums(dv),
        column_sums(branch_one),
        far_query_shift,
        far_value_shift,
        column_sums(branch_two),
        column_sums(up),
    ]
    small = jnp.concatenate([table_grad, jnp.stack(rows), expand_bias_grad], axis=0)
    small = sum_all(small, order_b, sizes)
    wide = lambda s: jnp.concatenate([s[i] for i in range(s.shape[0])], axis=1).astype(F32)
    return (
        result,
        input_gradient,
        memory_gradient,
        small[:steps],
        small[steps : steps + 3],
        small[steps + 3 : steps + 13],
        wide(entry_sum[1:]),
        entry_sum[0].astype(F32),
        cross_sum[1].astype(F32),
        wide(cross_sum[2:]),
        cross_sum[0].astype(F32),
        wide(expand_sum),
        small[steps + 13 :].reshape(-1),
        reduce_sum.reshape(-1, d).astype(F32),
    )


def solution(mesh):
    sizes = dict(mesh.shape)
    rows = P("dp", "seq", None)
    return jax.shard_map(
        functools.partial(on_device, sizes),
        mesh=mesh,
        in_specs=(rows, rows, P("dp"), rows) + (P(),) * 11,
        out_specs=(rows, rows, rows) + (P(),) * 11,
        check_vma=False,
    )
```

time: 630 us -> 347 us (0.55)
  waiting for transfers between devices: 292 us -> 80.8 us
  matrix products: 146 us -> 57 us
  starting transfers between devices: 0.9 us -> 54.7 us
  local copies, waits for them, and re-layouts: 82.7 us -> 35.2 us
  Pallas kernels: 0 us -> 46.3 us
  blocking collectives: 42.5 us -> 0 us
  other arithmetic: 46.4 us -> 64.3 us
  between operations: 14.7 us -> 4.38 us
    psum x1 -> x0, waiting for transfers between devices: 227 us -> none  [on_device(): lax.psum((table_grad, gains_grad, shifts_grad, entry_grad, self_exit_grad...]
    dot_general x35 -> x31, matrix products: 146 us -> 57 us  [dot(): return lax.dot_general(left, right, dims, preferred_element_type=F32)]
    ppermute x0 -> x55, waiting for transfers between devices: none -> 80.8 us  [the longest x49 79.4 us: swap(): return lax.ppermute(value, axis, [(i, i ^ 1 << bit) for i in range(size)])]
    ppermute x0 -> x55, starting transfers between devices: none -> 54.7 us  [the longest x49 45.8 us: swap(): return lax.ppermute(value, axis, [(i, i ^ 1 << bit) for i in range(size)])]
    pallas_call x0 -> x4, Pallas kernels: none -> 46.3 us  [the longest x2 26 us: attend_back(): pl.pallas_call(functools.partial(attend_back_body, nk // 2), grid=(pairs,...]
    psum x1 -> x0, blocking collectives: 42.5 us -> none  [on_device(): lax.psum((table_grad, gains_grad, shifts_grad, entry_grad, self_exit_grad...]
    all_gather x4 -> x0, waiting for transfers between devices: 40 us -> none  [the longest x1 15.5 us: on_device(): lax.all_gather(keys_local, 'seq', axis=1, tiled=True)]
    unnamed x141 -> x162, local copies, waits for them, and re-layouts: 36.3 us -> 8.67 us
  transfers between devices with their start and end apart: 9 -> 55, of which waited for: 6 -> 29; matrix products, arithmetic and copies ran while one was open for 27% -> 26% of each run, Pallas kernels for 0% -> 6%
where the time goes in v1:
time: 347 us; the launch traced here: 343 us
  waiting for transfers between devices  80.8 us (23%)
  other arithmetic  64.3 us (19%)
  matrix products  57 us (16%)
  starting transfers between devices  54.7 us (16%)
  Pallas kernels  46.3 us (13%)
  local copies, waits for them, and re-layouts  35.2 us (10%)
  between operations  4.38 us (1%)
    ppermute x49, waiting for transfers between devices, swap(): return lax.ppermute(value, axis, [(i, i ^ 1 << bit) for i in range(size)])  79.4 us
    dot_general x31, matrix products, dot(): return lax.dot_general(left, right, dims, preferred_element_type=F32)  57 us
    ppermute x49, starting transfers between devices, swap(): return lax.ppermute(value, axis, [(i, i ^ 1 << bit) for i in range(size)])  45.8 us
    pallas_call x2, Pallas kernels, attend_back(): pl.pallas_call(functools.partial(attend_back_body, nk // 2), grid=(pairs,...  26 us
    pallas_call x2, Pallas kernels, attend(): pl.pallas_call(attend_body, grid=(pairs,), in_specs=[row(nq), row(nk), ro...  20.3 us
    select_n x20, other arithmetic, reduce_all(): jnp.where(mine == 0, jnp.concatenate([value, got], axis=1), jnp.concatena...  13 us
    reduce_sum x6, other arithmetic, column_sums(): return jnp.sum(rows.astype(F32), axis=0)  9.53 us
    unnamed x162, local copies, waits for them, and re-layouts  8.67 us
  transfers between devices with their start and end apart: 55, of which 29 were waited for; matrix products, arithmetic and copies ran while one was open for 26% of the time, Pallas kernels for 6%

profile of v1, /device:TPU:0, one launch (start us, length us, event | category | flops | bytes accessed | tf_op | source)
XLA Modules:
  0.0 342.6 jit_solution(832360277540832337)
XLA Ops:
  3.0 3.1 collective-permute-start
  27.3 10.2 %attend.2 = (bf16[512,512]{1,0:T(8,128)(2,1)}, f32[4,2,512]{2,1,0:T(2,128)}) custom-call(bf16[512,512]{1,0:T(8,128)(2,1)} %fusion.18.q_ref, bf16[1024,512]{1,0:T(8,128)(2,1)} %slice.346.k_ref, bf16[1024,512]{1,0:T(8,128)(2,1)} %fusion.8.v_ref), custom_call_target="tpu_custom_call" | custom-call | flops 4294967296 | bytes 3145728 | tf_op jit(solution)/shard_map/attend/pallas_call | solution.py:72
  46.3 10.1 %attend.3 = (bf16[512,512]{1,0:T(8,128)(2,1)}, f32[4,2,512]{2,1,0:T(2,128)}) custom-call(bf16[512,512]{1,0:T(8,128)(2,1)} %fusion.17.q_ref, bf16[1024,512]{1,0:T(8,128)(2,1)} %slice.345.k_ref, bf16[1024,512]{1,0:T(8,128)(2,1)} %fusion.7.v_ref), custom_call_target="tpu_custom_call" | custom-call | flops 4294967296 | bytes 3145728 | tf_op jit(solution)/shard_map/attend/pallas_call | solution.py:72
  65.0 5.2 %convert_reduce_fusion = (f32[2048]{0:T(1024)S(1)}, bf16[512,2048]{1,0:T(8,128)(2,1)S(1)}) fusion(f32[512,2048]{1,0:T(8,128)S(1)} %fusion.65, f32[2048]{0:T(1024)S(1)} %copy-done.77, bf16[2048,512]{1,0:T(8,128)(2,1)S(1)} %copy-done, bf16[256,512]{0,1:T(8,128)(2,1)} %collective-permute-done.5, bf16[256,512]{0,1:T(8,128)(2,1)S(1)} %bitcast.162), kind=kOutput, calls=%fused_computation.9 | convolution fusion | flops 1098905600 | bytes 8929280 | tf_op jit(solution)/shard_map/dot_general | solution.py:23
  75.2 2.8 fusion.64
  86.0 12.9 %attend_back.2 = (bf16[512,512]{1,0:T(8,128)(2,1)}, bf16[1024,512]{1,0:T(8,128)(2,1)}, bf16[1024,512]{1,0:T(8,128)(2,1)}) custom-call(bf16[512,512]{1,0:T(8,128)(2,1)} %fusion.17.q_ref, bf16[1024,512]{1,0:T(8,128)(2,1)} %slice.345.k_ref, bf16[1024,512]{1,0:T(8,128)(2,1)} %fusion.7.v_ref, bf16[512,512]{1,0:T(8,128)(2,1)} %get-tuple-element.25.o_ref, ...), custom_call_target="tpu_custom_call" | custom-call | flops 10737418240 | bytes 4718592 | tf_op jit(solution)/shard_map/attend_back/pallas_call | solution.py:128
  112.4 13.1 %attend_back.3 = (bf16[512,512]{1,0:T(8,128)(2,1)}, bf16[1024,512]{1,0:T(8,128)(2,1)}, bf16[1024,512]{1,0:T(8,128)(2,1)}) custom-call(bf16[512,512]{1,0:T(8,128)(2,1)} %fusion.18.q_ref, bf16[1024,512]{1,0:T(8,128)(2,1)} %slice.346.k_ref, bf16[1024,512]{1,0:T(8,128)(2,1)} %fusion.8.v_ref, bf16[512,512]{1,0:T(8,128)(2,1)} %get-tuple-element.24.o_ref, ...), custom_call_target="tpu_custom_call" | custom-call | flops 10737418240 | bytes 4718592 | tf_op jit(solution)/shard_map/attend_back/pallas_call | solution.py:128
  127.7 2.8 fusion.14
  139.8 5.0 %multiply_reduce_fusion = (f32[512]{0:T(512)S(1)}, f32[1024]{0:T(1024)S(1)}, f32[1024]{0:T(1024)S(1)}, f32[512]{0:T(512)S(1)}, f32[1024,512]{0,1:T(8,128)}) fusion(f32[1024]{0:T(1024)S(1)} %add_rsqrt_fusion, f32[1024]{0:T(1024)S(1)} %broadcast_multiply_fusion.3, bf16[512,512]{0,1:T(8,128)(2,1)S(1)} %copy-done.5, bf16[256,512]{0,1:T(8,128)(2,1)S(1)} %copy-done.8, ...), kind=kOutput, calls=%fused_computation.33 | convolution fusion | flops 545780736 | bytes 7886848 | tf_op jit(solution)/shard_map/dot_general | solution.py:23
  160.0 3.2 convolution_convert_fusion
  170.6 4.4 %collective-permute-done.11 = f32[67,512]{1,0:T(8,128)S(1)} collective-permute-done((f32[67,512]{1,0:T(8,128)S(1)}, f32[67,512]{1,0:T(8,128)S(1)}, u32[]{:S(2)}, u32[]{:S(2)}) %collective-permute-start.11) | collective-permute-done | bytes 137248 | tf_op jit(solution)/shard_map/ppermute | solution.py:153
  177.9 3.5 %collective-permute-done.12 = f32[67,512]{1,0:T(8,128)S(1)} collective-permute-done((f32[67,512]{1,0:T(8,128)S(1)}, f32[67,512]{1,0:T(8,128)S(1)}, u32[]{:S(2)}, u32[]{:S(2)}) %collective-permute-start.12) | collective-permute-done | bytes 137248 | tf_op jit(solution)/shard_map/ppermute | solution.py:153
  186.6 2.9 collective-permute-done.13
  193.8 4.8 %collective-permute-done.14 = f32[67,512]{1,0:T(8,128)S(1)} collective-permute-done((f32[67,512]{1,0:T(8,128)S(1)}, f32[67,512]{1,0:T(8,128)S(1)}, u32[]{:S(2)}, u32[]{:S(2)}) %collective-permute-start.14) | collective-permute-done | bytes 137248 | tf_op jit(solution)/shard_map/ppermute | solution.py:153
  212.1 5.7 %collective-permute-done.46 = bf16[4,128,512]{2,1,0:T(8,128)(2,1)S(1)} collective-permute-done((bf16[4,128,512]{2,1,0:T(8,128)(2,1)S(1)}, bf16[4,128,512]{2,1,0:T(8,128)(2,1)S(1)}, u32[]{:S(2)}, u32[]{:S(2)}) %collective-permute-start.46) | collective-permute-done | bytes 524320 | tf_op jit(solution)/shard_map/ppermute | solution.py:153
  221.8 7.2 %collective-permute-done.26 = bf16[4,128,512]{2,1,0:T(8,128)(2,1)S(1)} collective-permute-done((bf16[4,128,512]{2,1,0:T(8,128)(2,1)S(1)}, bf16[4,128,512]{2,1,0:T(8,128)(2,1)S(1)}, u32[]{:S(2)}, u32[]{:S(2)}) %collective-permute-start.26) | collective-permute-done | bytes 524320 | tf_op jit(solution)/shard_map/ppermute | solution.py:153
  233.0 4.8 %collective-permute-done.47 = bf16[4,64,512]{2,1,0:T(8,128)(2,1)S(1)} collective-permute-done((bf16[4,64,512]{2,1,0:T(8,128)(2,1)S(1)}, bf16[4,64,512]{2,1,0:T(8,128)(2,1)S(1)}, u32[]{:S(2)}, u32[]{:S(2)}) %collective-permute-start.47) | collective-permute-done | bytes 262176 | tf_op jit(solution)/shard_map/ppermute | solution.py:153
  243.8 2.8 collective-permute-start.49
  257.7 4.3 %collective-permute-done.29 = bf16[4,16,512]{2,1,0:T(8,128)(2,1)S(1)} collective-permute-done((bf16[4,16,512]{2,1,0:T(8,128)(2,1)S(1)}, bf16[4,16,512]{2,1,0:T(8,128)(2,1)S(1)}, u32[]{:S(2)}, u32[]{:S(2)}) %collective-permute-start.29) | collective-permute-done | bytes 65568 | tf_op jit(solution)/shard_map/ppermute | solution.py:153
  291.1 6.1 %collective-permute-done.43 = bf16[4,128,512]{2,1,0:T(8,128)(2,1)S(1)} collective-permute-done((bf16[4,128,512]{2,1,0:T(8,128)(2,1)S(1)}, bf16[4,128,512]{2,1,0:T(8,128)(2,1)S(1)}, u32[]{:S(2)}, u32[]{:S(2)}) %collective-permute-start.43) | collective-permute-done | bytes 524320 | tf_op jit(solution)/shard_map/ppermute | solution.py:153
  299.0 3.9 %collective-permute-done.52 = bf16[4,64,512]{2,1,0:T(8,128)(2,1)S(1)} collective-permute-done((bf16[4,64,512]{2,1,0:T(8,128)(2,1)S(1)}, bf16[4,64,512]{2,1,0:T(8,128)(2,1)S(1)}, u32[]{:S(2)}, u32[]{:S(2)}) %collective-permute-start.52) | collective-permute-done | bytes 262176 | tf_op jit(solution)/shard_map/ppermute | solution.py:153
  305.3 8.9 %collective-permute-done.23 = bf16[4,128,512]{2,1,0:T(8,128)(2,1)S(1)} collective-permute-done((bf16[4,128,512]{2,1,0:T(8,128)(2,1)S(1)}, bf16[4,128,512]{2,1,0:T(8,128)(2,1)S(1)}, u32[]{:S(2)}, u32[]{:S(2)}) %collective-permute-start.23) | collective-permute-done | bytes 524320 | tf_op jit(solution)/shard_map/ppermute | solution.py:153
  326.8 2.9 maximum_select_fusion
  333.4 2.7 bitcast_convert_fusion
  (435 shorter events, 205.0 us)
Async XLA Ops:
  8.7 56.3 %collective-permute-start.5 = (bf16[256,512]{0,1:T(8,128)(2,1)}, bf16[256,512]{0,1:T(8,128)(2,1)}, u32[]{:S(2)}, u32[]{:S(2)}) collective-permute-start(bf16[256,512]{0,1:T(8,128)(2,1)} %bitcast.22), channel_id=1, source_target_pairs={{0,2},{1,3},{2,0},{3,1},{4,6},{5,7},{6,4},{7,5},{8,10},{9,11},{10,... | collective-permute-start | bytes 786440 | tf_op jit(solution)/shard_map/ppermute | solution.py:166
  20.7 18.7 %collective-permute-start.3 = (bf16[512,512]{1,0:T(8,128)(2,1)}, bf16[512,512]{1,0:T(8,128)(2,1)}, u32[]{:S(2)}, u32[]{:S(2)}) collective-permute-start(bf16[512,512]{1,0:T(8,128)(2,1)} %pad_maximum_fusion.6), channel_id=1, source_target_pairs={{0,1},{1,0},{2,3},{3,2},{4,5},{5,4},{6,7},{7,6},{8,9},{9,8},{10,11... | collective-permute-start | bytes 1572872 | tf_op jit(solution)/shard_map/ppermute | solution.py:153
  137.4 37.6 %collective-permute-start.4 = (bf16[256,512]{0,1:T(8,128)(2,1)}, bf16[256,512]{0,1:T(8,128)(2,1)}, u32[]{:S(2)}, u32[]{:S(2)}) collective-permute-start(bf16[256,512]{0,1:T(8,128)(2,1)} %slice.351), channel_id=1, source_target_pairs={{0,2},{1,3},{2,0},{3,1},{4,6},{5,7},{6,4},{7,5},{8,10},{9,11},{10,... | collective-permute-start | bytes 786440 | tf_op jit(solution)/shard_map/ppermute | solution.py:178
  145.1 23.0 %collective-permute-start.10 = (f32[67,512]{1,0:T(8,128)S(1)}, f32[67,512]{1,0:T(8,128)}, u32[]{:S(2)}, u32[]{:S(2)}) collective-permute-start(f32[67,512]{1,0:T(8,128)S(1)} %concatenate.158), channel_id=1, source_target_pairs={{0,1},{1,0},{2,3},{3,2},{4,5},{5,4},{6,7},{7,6},{8,9},{9,8},{10,11... | collective-permute-start | bytes 411656 | tf_op jit(solution)/shard_map/ppermute | solution.py:153
  148.6 32.8 %collective-permute-start.6 = (bf16[512,512]{0,1:T(8,128)(2,1)}, bf16[512,512]{0,1:T(8,128)(2,1)}, u32[]{:S(2)}, u32[]{:S(2)}) collective-permute-start(bf16[512,512]{0,1:T(8,128)(2,1)} %slice.348), channel_id=1, source_target_pairs={{0,1},{1,0},{2,3},{3,2},{4,5},{5,4},{6,7},{7,6},{8,9},{9,8},{10,11... | collective-permute-start | bytes 1572872 | tf_op jit(solution)/shard_map/ppermute | solution.py:153
  159.1 24.5 %collective-permute-start.8 = (bf16[512,512]{1,0:T(8,128)(2,1)}, bf16[512,512]{1,0:T(8,128)(2,1)}, u32[]{:S(2)}, u32[]{:S(2)}) collective-permute-start(bf16[512,512]{1,0:T(8,128)(2,1)} %slice.347), channel_id=1, source_target_pairs={{0,1},{1,0},{2,3},{3,2},{4,5},{5,4},{6,7},{7,6},{8,9},{9,8},{10,11... | collective-permute-start | bytes 1572872 | tf_op jit(solution)/shard_map/ppermute | solution.py:153
  165.6 35.3 %collective-permute-start.45 = (bf16[4,256,512]{2,1,0:T(8,128)(2,1)}, bf16[4,256,512]{2,1,0:T(8,128)(2,1)}, u32[]{:S(2)}, u32[]{:S(2)}) collective-permute-start(bf16[4,256,512]{2,1,0:T(8,128)(2,1)} %constant_dynamic-slice_fusion.4), channel_id=1, source_target_pairs={{0,1},{1,0},{2,3},{3,2},{4,5},{5,4},{6,7},{7,6},{8,9},{9,8},{10,11... | collective-permute-start | bytes 3145736 | tf_op jit(solution)/shard_map/ppermute | solution.py:153
  175.0 29.6 %collective-permute-start.35 = (bf16[4,256,512]{2,1,0:T(8,128)(2,1)}, bf16[4,256,512]{2,1,0:T(8,128)(2,1)}, u32[]{:S(2)}, u32[]{:S(2)}) collective-permute-start(bf16[4,256,512]{2,1,0:T(8,128)(2,1)} %constant_dynamic-slice_fusion.9), channel_id=1, source_target_pairs={{0,1},{1,0},{2,3},{3,2},{4,5},{5,4},{6,7},{7,6},{8,9},{9,8},{10,11... | collective-permute-start | bytes 3145736 | tf_op jit(solution)/shard_map/ppermute | solution.py:153
  181.4 26.4 %collective-permute-start.25 = (bf16[4,256,512]{2,1,0:T(8,128)(2,1)}, bf16[4,256,512]{2,1,0:T(8,128)(2,1)}, u32[]{:S(2)}, u32[]{:S(2)}) collective-permute-start(bf16[4,256,512]{2,1,0:T(8,128)(2,1)} %constant_dynamic-slice_fusion.14), channel_id=1, source_target_pairs={{0,1},{1,0},{2,3},{3,2},{4,5},{5,4},{6,7},{7,6},{8,9},{9,8},{10,11... | collective-permute-start | bytes 3145736 | tf_op jit(solution)/shard_map/ppermute | solution.py:153
  181.4 28.5 %collective-permute-start.15 = (bf16[4,256,512]{2,1,0:T(8,128)(2,1)}, bf16[4,256,512]{2,1,0:T(8,128)(2,1)}, u32[]{:S(2)}, u32[]{:S(2)}) collective-permute-start(bf16[4,256,512]{2,1,0:T(8,128)(2,1)} %constant_dynamic-slice_fusion.19), channel_id=1, source_target_pairs={{0,1},{1,0},{2,3},{3,2},{4,5},{5,4},{6,7},{7,6},{8,9},{9,8},{10,11... | collective-permute-start | bytes 3145736 | tf_op jit(solution)/shard_map/ppermute | solution.py:153
  198.5 117.0 %collective-permute-start.7 = (bf16[256,512]{0,1:T(8,128)(2,1)S(1)}, bf16[256,512]{0,1:T(8,128)(2,1)S(1)}, u32[]{:S(2)}, u32[]{:S(2)}) collective-permute-start(bf16[256,512]{0,1:T(8,128)(2,1)S(1)} %slice.350), channel_id=1, source_target_pairs={{0,2},{1,3},{2,0},{3,1},{4,6},{5,7},{6,4},{7,5},{8,10},{9,11},{10,... | collective-permute-start | bytes 786440 | tf_op jit(solution)/shard_map/ppermute | solution.py:178
  206.1 14.9 %collective-permute-start.36 = (bf16[4,128,512]{2,1,0:T(8,128)(2,1)S(1)}, bf16[4,128,512]{2,1,0:T(8,128)(2,1)S(1)}, u32[]{:S(2)}, u32[]{:S(2)}) collective-permute-start(bf16[4,128,512]{2,1,0:T(8,128)(2,1)S(1)} %constant_dynamic-slice_fusion.8), channel_id=1, source_target_pairs={{0,2},{1,3},{2,0},{3,1},{4,6},{5,7},{6,4},{7,5},{8,10},{9,11},{10,... | collective-permute-start | bytes 1572872 | tf_op jit(solution)/shard_map/ppermute | solution.py:153
  209.3 19.7 %collective-permute-start.26 = (bf16[4,128,512]{2,1,0:T(8,128)(2,1)S(1)}, bf16[4,128,512]{2,1,0:T(8,128)(2,1)S(1)}, u32[]{:S(2)}, u32[]{:S(2)}) collective-permute-start(bf16[4,128,512]{2,1,0:T(8,128)(2,1)S(1)} %constant_dynamic-slice_fusion.13), channel_id=1, source_target_pairs={{0,4},{4,0},{8,12},{12,8},{16,20},{20,16},{24,28},{28,24},{1,5},{5... | collective-permute-start | bytes 1572872 | tf_op jit(solution)/shard_map/ppermute | solution.py:153
  211.5 20.7 %collective-permute-start.16 = (bf16[4,128,512]{2,1,0:T(8,128)(2,1)S(1)}, bf16[4,128,512]{2,1,0:T(8,128)(2,1)S(1)}, u32[]{:S(2)}, u32[]{:S(2)}) collective-permute-start(bf16[4,128,512]{2,1,0:T(8,128)(2,1)S(1)} %constant_dynamic-slice_fusion.18), channel_id=1, source_target_pairs={{0,2},{1,3},{2,0},{3,1},{4,6},{5,7},{6,4},{7,5},{8,10},{9,11},{10,... | collective-permute-start | bytes 1572872 | tf_op jit(solution)/shard_map/ppermute | solution.py:153
  218.0 19.9 %collective-permute-start.47 = (bf16[4,64,512]{2,1,0:T(8,128)(2,1)S(1)}, bf16[4,64,512]{2,1,0:T(8,128)(2,1)S(1)}, u32[]{:S(2)}, u32[]{:S(2)}) collective-permute-start(bf16[4,64,512]{2,1,0:T(8,128)(2,1)S(1)} %constant_dynamic-slice_fusion.2), channel_id=1, source_target_pairs={{0,2},{1,3},{2,0},{3,1},{4,6},{5,7},{6,4},{7,5},{8,10},{9,11},{10,... | collective-permute-start | bytes 786440 | tf_op jit(solution)/shard_map/ppermute | solution.py:153
  221.2 17.5 %collective-permute-start.37 = (bf16[4,64,512]{2,1,0:T(8,128)(2,1)S(1)}, bf16[4,64,512]{2,1,0:T(8,128)(2,1)S(1)}, u32[]{:S(2)}, u32[]{:S(2)}) collective-permute-start(bf16[4,64,512]{2,1,0:T(8,128)(2,1)S(1)} %constant_dynamic-slice_fusion.7), channel_id=1, source_target_pairs={{0,4},{4,0},{8,12},{12,8},{16,20},{20,16},{24,28},{28,24},{1,5},{5... | collective-permute-start | bytes 786440 | tf_op jit(solution)/shard_map/ppermute | solution.py:153
  254.6 21.0 %collective-permute-start.50 = (bf16[4,16,512]{2,1,0:T(8,128)(2,1)S(1)}, bf16[4,16,512]{2,1,0:T(8,128)(2,1)S(1)}, u32[]{:S(2)}, u32[]{:S(2)}) collective-permute-start(bf16[4,16,512]{2,1,0:T(8,128)(2,1)S(1)} %add_convert_fusion.19), channel_id=1, source_target_pairs={{0,16},{4,20},{8,24},{12,28},{16,0},{20,4},{24,8},{28,12},{1,17},{... | collective-permute-start | bytes 196616 | tf_op jit(solution)/shard_map/ppermute | solution.py:153
  282.2 15.1 %collective-permute-start.43 = (bf16[4,128,512]{2,1,0:T(8,128)(2,1)S(1)}, bf16[4,128,512]{2,1,0:T(8,128)(2,1)S(1)}, u32[]{:S(2)}, u32[]{:S(2)}) collective-permute-start(bf16[4,128,512]{2,1,0:T(8,128)(2,1)S(1)} %maximum_select_fusion.10), channel_id=1, source_target_pairs={{0,2},{1,3},{2,0},{3,1},{4,6},{5,7},{6,4},{7,5},{8,10},{9,11},{10,... | collective-permute-start | bytes 1572872 | tf_op jit(solution)/shard_map/ppermute | solution.py:153
  283.8 19.1 %collective-permute-start.52 = (bf16[4,64,512]{2,1,0:T(8,128)(2,1)S(1)}, bf16[4,64,512]{2,1,0:T(8,128)(2,1)S(1)}, u32[]{:S(2)}, u32[]{:S(2)}) collective-permute-start(bf16[4,64,512]{2,1,0:T(8,128)(2,1)S(1)} %maximum_select_fusion.15), channel_id=1, source_target_pairs={{0,2},{1,3},{2,0},{3,1},{4,6},{5,7},{6,4},{7,5},{8,10},{9,11},{10,... | collective-permute-start | bytes 786440 | tf_op jit(solution)/shard_map/ppermute | solution.py:153
  286.3 16.9 %collective-permute-start.33 = (bf16[4,128,512]{2,1,0:T(8,128)(2,1)S(1)}, bf16[4,128,512]{2,1,0:T(8,128)(2,1)S(1)}, u32[]{:S(2)}, u32[]{:S(2)}) collective-permute-start(bf16[4,128,512]{2,1,0:T(8,128)(2,1)S(1)} %maximum_select_fusion.9), channel_id=1, source_target_pairs={{0,4},{4,0},{8,12},{12,8},{16,20},{20,16},{24,28},{28,24},{1,5},{5... | collective-permute-start | bytes 1572872 | tf_op jit(solution)/shard_map/ppermute | solution.py:153
  289.0 25.2 %collective-permute-start.23 = (bf16[4,128,512]{2,1,0:T(8,128)(2,1)S(1)}, bf16[4,128,512]{2,1,0:T(8,128)(2,1)S(1)}, u32[]{:S(2)}, u32[]{:S(2)}) collective-permute-start(bf16[4,128,512]{2,1,0:T(8,128)(2,1)S(1)} %maximum_select_fusion.8), channel_id=1, source_target_pairs={{0,2},{1,3},{2,0},{3,1},{4,6},{5,7},{6,4},{7,5},{8,10},{9,11},{10,... | collective-permute-start | bytes 1572872 | tf_op jit(solution)/shard_map/ppermute | solution.py:153
  297.3 21.7 %collective-permute-start.9 = (bf16[256,512]{1,0:T(8,128)(2,1)S(1)}, bf16[256,512]{1,0:T(8,128)(2,1)}, u32[]{:S(2)}, u32[]{:S(2)}) collective-permute-start(bf16[256,512]{1,0:T(8,128)(2,1)S(1)} %slice.349), channel_id=1, source_target_pairs={{0,2},{1,3},{2,0},{3,1},{4,6},{5,7},{6,4},{7,5},{8,10},{9,11},{10,... | collective-permute-start | bytes 786440 | tf_op jit(solution)/shard_map/ppermute | solution.py:178
  302.9 19.5 %collective-permute-start.44 = (bf16[4,256,512]{2,1,0:T(8,128)(2,1)S(1)}, bf16[4,256,512]{2,1,0:T(8,128)(2,1)}, u32[]{:S(2)}, u32[]{:S(2)}) collective-permute-start(bf16[4,256,512]{2,1,0:T(8,128)(2,1)S(1)} %maximum_select_fusion.6), channel_id=1, source_target_pairs={{0,1},{1,0},{2,3},{3,2},{4,5},{5,4},{6,7},{7,6},{8,9},{9,8},{10,11... | collective-permute-start | bytes 3145736 | tf_op jit(solution)/shard_map/ppermute | solution.py:153
  303.1 17.6 %collective-permute-start.53 = (bf16[4,128,512]{2,1,0:T(8,128)(2,1)S(1)}, bf16[4,128,512]{2,1,0:T(8,128)(2,1)}, u32[]{:S(2)}, u32[]{:S(2)}) collective-permute-start(bf16[4,128,512]{2,1,0:T(8,128)(2,1)S(1)} %maximum_select_fusion.11), channel_id=1, source_target_pairs={{0,4},{4,0},{8,12},{12,8},{16,20},{20,16},{24,28},{28,24},{1,5},{5... | collective-permute-start | bytes 1572872 | tf_op jit(solution)/shard_map/ppermute | solution.py:153
  (111 other events, 1025.5 us)
